TPU v7x, 32 devices: a whole 2x2x4 slice. The times are simulated.
32 devices in a mesh: league: 4 (over x, core), env: 8 (over z, y).
Axes of the slice: x: 2, y: 2, z: 4, core: 2. Of those that a mesh axis runs over, the one named last changes fastest.
Arguments:
- obs_own: bfloat16 [4, 2, 128, 16, 2048], P('league', None, 'env'), may hold values from -6 to 6
- obs_opp: bfloat16 [4, 2, 128, 16, 2048], P('league', None, 'env'), may hold values from -6 to 6
- actions: int32 [4, 2, 2, 128, 16], P('league', None, None, 'env'), may hold values from 0 to 255
- opponent_picks: int32 [4, 2], P('league'), may hold values from 0 to 3
- policy_weight: bfloat16 [4, 2048, 2048], P('league', 'env'), may hold values from -0.125 to 0.125
- policy_gain: bfloat16 [4, 2048], P('league'), may hold values from 0.25 to 1.75
- action_table: bfloat16 [256, 2048], replicated, may hold values from -6 to 6
- value_gain: bfloat16 [2048], replicated, may hold values from 0.25 to 1.75
- value_up: bfloat16 [2048, 1024], replicated, may hold values from -0.125 to 0.125
- value_out: bfloat16 [1024], replicated, may hold values from -0.1875 to 0.1875
Outputs:
- learner_rows: bfloat16 [4, 2, 16, 2048, 128], P('league', None, None, 'env')
- values: float32 [4, 2, 128, 16], P('league', None, 'env')
All inputs are finite; a program needn't handle non-finite values.
Results may differ from a plain program's by a relative error of at most 0.0054.
Values may be sent and summed in bfloat16 or wider, within the bound.
A program may use at most 128 MiB of HBM per device.

v0:
```python
import jax
import jax.numpy as jnp
from jax import lax
from jax.sharding import PartitionSpec as P


def rms_norm(inputs, gain):
    scale = lax.rsqrt(jnp.mean(inputs * inputs, axis=-1, keepdims=True) + 1e-05)
    return inputs * scale * gain.astype(jnp.float32)


def local(
    obs_own,
    obs_opp,
    actions,
    opponent_picks,
    policy_weight,
    policy_gain,
    action_table,
    value_gain,
    value_up,
    value_out,
):
    round_count = obs_own.shape[1]
    env_count = obs_own.shape[2]
    step_count = obs_own.shape[3]
    model_width = obs_own.shape[4]
    row_count = env_count * step_count
    weight_shard = policy_weight[0]
    own_gain = policy_gain[0]
    group_count = lax.axis_size("league")
    my_group = lax.axis_index("league")
    own_inputs = obs_own[0].reshape(round_count * row_count, model_width).astype(jnp.float32)
    own_normed = rms_norm(own_inputs, own_gain).astype(jnp.bfloat16)
    own_whole = lax.all_gather(weight_shard, "env", axis=0, tiled=True)
    own_state = own_inputs + jnp.dot(own_normed, own_whole, preferred_element_type=jnp.float32)
    every_pick = lax.all_gather(opponent_picks, "league", axis=0, tiled=True)
    action_range = jnp.arange(action_table.shape[0], dtype=jnp.int32)
    traj_list = []
    value_list = []
    for round_index in range(round_count):
        opp_raw = obs_opp[0, round_index].reshape(row_count, model_width)
        opp_inputs = opp_raw.astype(jnp.float32)
        all_rows = lax.all_gather(opp_raw, "league", axis=0, tiled=True)
        all_normed = rms_norm(all_rows.astype(jnp.float32), own_gain).astype(jnp.bfloat16)
        products = jnp.dot(all_normed, own_whole, preferred_element_type=jnp.float32)
        served = (every_pick[:, round_index] == my_group).astype(jnp.float32)
        products = (
            products.reshape(group_count, row_count, model_width) * served[:, None, None]
        ).reshape(group_count * row_count, model_width)
        opp_state = opp_inputs + lax.psum_scatter(
            products, "league", scatter_dimension=0, tiled=True
        )
        own_ids = actions[0, 0, round_index].reshape(row_count)
        opp_ids = actions[0, 1, round_index].reshape(row_count)
        onehot = (own_ids[:, None] == action_range[None, :]).astype(jnp.bfloat16) + (
            opp_ids[:, None] == action_range[None, :]
        ).astype(jnp.bfloat16)
        action_sum = jnp.dot(onehot, action_table, preferred_element_type=jnp.float32)
        round_state = lax.dynamic_slice_in_dim(own_state, round_index * row_count, row_count, 0)
        joint_sum = round_state + opp_state + action_sum
        joint_row = rms_norm(joint_sum, value_gain).astype(jnp.bfloat16)
        value_hidden = jax.nn.silu(
            jnp.dot(joint_row, value_up, preferred_element_type=jnp.float32)
        ).astype(jnp.bfloat16)
        value_est = jnp.dot(value_hidden, value_out, preferred_element_type=jnp.float32)
        value_list.append(value_est.reshape(env_count, step_count))
        time_block = joint_row.reshape(env_count, step_count, model_width).transpose(1, 2, 0)
        traj_list.append(lax.all_to_all(time_block, "env", split_axis=1, concat_axis=2, tiled=True))
    learner_rows = jnp.stack(traj_list)
    values = jnp.stack(value_list)
    return (learner_rows[None], values[None])


def solution(mesh):
    in_specs = (
        P("league", None, "env", None, None),
        P("league", None, "env", None, None),
        P("league", None, None, "env", None),
        P("league", None),
        P("league", "env", None),
        P("league", None),
        P(),
        P(),
        P(),
        P(),
    )
    out_specs = (P("league", None, None, "env", None), P("league", None, "env", None))
    return jax.shard_map(local, mesh=mesh, in_specs=in_specs, out_specs=out_specs, check_vma=False)
```

profile of v0, /device:TPU:0, one launch (start us, length us, event | category | flops | bytes accessed | tf_op | source)
XLA Modules:
  0.0 480.6 jit_solution(18280044370628031255)
XLA Ops:
  12.0 6.0 %all-gather.1 = s32[4,1,2]{2,1,0:T(1,128)S(1)} all-gather(s32[1,1,2]{2,1,0:T(1,128)S(1)} %bitcast.98), channel_id=1, replica_groups=mesh['league'=4,'env'=8] {'league'}, dimensions={0}, use_global_device_ids=true | all-gather | bytes 40 | tf_op jit(solution)/shard_map/all_gather | solution.py:37
  18.2 29.6 %all-gather.6.cloned.1.call-done = bf16[1024,2048]{1,0:T(8,128)(2,1)} async-done(((bf16[256,2048]{1,0:T(8,128)(2,1)}), bf16[1024,2048]{1,0:T(8,128)(2,1)}) %all-gather.6.cloned.1.call-update) | async-done | bytes 4194320 | tf_op jit(solution)/shard_map/all_gather | solution.py:44
  50.9 124.0 %all-gather.10.cloned.1.call-done = bf16[1,2048,2048]{2,1,0:T(8,128)(2,1)} async-done(((bf16[1,256,2048]{2,1,0:T(8,128)(2,1)}), bf16[1,2048,2048]{2,1,0:T(8,128)(2,1)}) %all-gather.10.cloned.1.call-update) | async-done | bytes 8388624 | tf_op jit(solution)/shard_map/all_gather | solution.py:35
  174.9 14.5 %fusion.12 = f32[1024,2048]{1,0:T(8,128)} fusion(bf16[1,2048,2048]{2,1,0:T(8,128)(2,1)} %all-gather.10.cloned.1.call-done, bf16[1024,2048]{1,0:T(8,128)(2,1)} %all-gather.6.cloned.1.call-done, f32[1024]{0:T(1024)S(1)} %bitcast.94, f32[2048]{0:T(1024)S(1)} %bitcast.90, f32[1024]{0:T(1024)S(1)} %add_rsqrt_fusion.2), kind=kOutput, calls=%fused_computation.16 | convolution fusion | flops 8600420352 | bytes 20987904 | tf_op jit(solution)/shard_map/dot_general | solution.py:46
  189.7 19.5 %all-gather.8.cloned.1.call-done = bf16[1024,2048]{1,0:T(8,128)(2,1)} async-done(((bf16[256,2048]{1,0:T(8,128)(2,1)}), bf16[1024,2048]{1,0:T(8,128)(2,1)}) %all-gather.8.cloned.1.call-update) | async-done | bytes 4194320 | tf_op jit(solution)/shard_map/all_gather | solution.py:44
  212.6 13.6 %fusion.15 = f32[1024,2048]{1,0:T(8,128)} fusion(bf16[1,2048,2048]{2,1,0:T(8,128)(2,1)} %all-gather.10.cloned.1.call-done, bf16[1024,2048]{1,0:T(8,128)(2,1)S(1)} %copy-done.6, f32[1024]{0:T(1024)S(1)} %bitcast.95, f32[1024]{0:T(1024)S(1)} %add_rsqrt_fusion.1, f32[2048]{0:T(1024)S(1)} %bitcast.91), kind=kOutput, calls=%fused_computation.17 | convolution fusion | flops 8600420352 | bytes 20987904 | tf_op jit(solution)/shard_map/dot_general | solution.py:46
  230.2 9.6 %bitcast_add_fusion = f32[512,2048]{1,0:T(8,128)} fusion(bf16[1,2,16,16,2048]{4,3,2,1,0:T(8,128)(2,1)S(1)} %copy-done.5, bf16[512,2048]{1,0:T(8,128)(2,1)S(1)} %fusion.22, bf16[1,2048,2048]{2,1,0:T(8,128)(2,1)} %all-gather.10.cloned.1.call-done), kind=kOutput, calls=%fused_computation.18 | convolution fusion | flops 4297064448 | bytes 16777216 | tf_op jit(solution)/shard_map/dot_general | solution.py:36
  239.9 43.5 %reduce-scatter.3.cloned.1.call-done = f32[256,2048]{1,0:T(8,128)} async-done(((f32[1024,2048]{1,0:T(8,128)}), f32[256,2048]{1,0:T(8,128)}) %reduce-scatter.3.cloned.1.call-update) | async-done | bytes 2097168 | tf_op jit(solution)/shard_map/reduce_scatter | solution.py:51
  283.4 4.2 multiply_reduce_fusion.1
  287.6 70.1 %reduce-scatter.5.cloned.1.call-done = f32[256,2048]{1,0:T(8,128)} async-done(((f32[1024,2048]{1,0:T(8,128)}), f32[256,2048]{1,0:T(8,128)}) %reduce-scatter.5.cloned.1.call-update) | async-done | bytes 2097168 | tf_op jit(solution)/shard_map/reduce_scatter | solution.py:51
  361.3 8.8 %copy.27 = bf16[16,16,2048]{0,1,2:T(8,128)(2,1)} copy(bf16[16,16,2048]{2,1,0:T(8,128)(2,1)S(1)} %bitcast.87) | data formatting | bytes 2097152 | tf_op jit(solution)/shard_map/reshape | solution.py:68
  370.1 7.5 %bitcast_bitcast_fusion = bf16[2048,16,16]{2,1,0:T(8,128)(2,1)} fusion(bf16[16,16,2048]{0,1,2:T(8,128)(2,1)} %copy.27), kind=kLoop, calls=%fused_computation.71 | loop fusion | bytes 2097152
  377.6 11.2 %reshape.107 = bf16[8,2,32768]{2,1,0:T(2,128)(2,1)} reshape(bf16[2048,16,16]{2,1,0:T(8,128)(2,1)} %bitcast_bitcast_fusion) | data formatting | bytes 2097152
  388.8 5.5 %all-to-all-start.1 = ((bf16[8,2,32768]{2,1,0:T(2,128)(2,1)}), bf16[8,2,32768]{2,1,0:T(2,128)(2,1)S(1)}, u32[]{:S(2)}, u32[]{:S(2)}) async-start(bf16[8,2,32768]{2,1,0:T(2,128)(2,1)} %reshape.107), calls=%async_computation.3 | async-start | bytes 2097152 | tf_op jit(solution)/shard_map/all_to_all | solution.py:69
  394.3 8.8 %copy.24 = bf16[16,16,2048]{0,1,2:T(8,128)(2,1)} copy(bf16[16,16,2048]{2,1,0:T(8,128)(2,1)S(1)} %bitcast.86) | data formatting | bytes 2097152 | tf_op jit(solution)/shard_map/reshape | solution.py:68
  403.1 7.5 %bitcast_bitcast_fusion.1 = bf16[2048,16,16]{2,1,0:T(8,128)(2,1)} fusion(bf16[16,16,2048]{0,1,2:T(8,128)(2,1)} %copy.24), kind=kLoop, calls=%fused_computation.72 | loop fusion | bytes 2097152
  410.6 11.2 %reshape.109 = bf16[8,2,32768]{2,1,0:T(2,128)(2,1)} reshape(bf16[2048,16,16]{2,1,0:T(8,128)(2,1)} %bitcast_bitcast_fusion.1) | data formatting | bytes 2097152
  421.8 6.0 %all-to-all-start = ((bf16[8,2,32768]{2,1,0:T(2,128)(2,1)}), bf16[8,2,32768]{2,1,0:T(2,128)(2,1)S(1)}, u32[]{:S(2)}, u32[]{:S(2)}) async-start(bf16[8,2,32768]{2,1,0:T(2,128)(2,1)} %reshape.109), calls=%async_computation.1 | async-start | bytes 2097152 | tf_op jit(solution)/shard_map/all_to_all | solution.py:69
  427.9 3.9 fusion.30
  431.9 4.0 fusion.29
  436.6 7.5 %reshape.108 = bf16[2048,16,16]{2,1,0:T(8,128)(2,1)} reshape(bf16[8,2,32768]{2,1,0:T(2,128)(2,1)S(1)} %all-to-all-done.1) | data formatting | bytes 2097152
  444.1 9.1 %copy.29 = bf16[16,256,8,16]{1,3,2,0:T(8,128)(2,1)} copy(bf16[16,256,8,16]{3,0,1,2:T(8,128)(2,1)} %bitcast.80) | data formatting | bytes 2097152 | tf_op jit(solution)/shard_map/all_to_all | solution.py:69
  453.3 7.5 %reshape.110 = bf16[2048,16,16]{2,1,0:T(8,128)(2,1)} reshape(bf16[8,2,32768]{2,1,0:T(2,128)(2,1)S(1)} %all-to-all-done) | data formatting | bytes 2097152
  460.8 9.1 %copy.26 = bf16[16,256,8,16]{1,3,2,0:T(8,128)(2,1)} copy(bf16[16,256,8,16]{3,0,1,2:T(8,128)(2,1)} %bitcast.81) | data formatting | bytes 2097152 | tf_op jit(solution)/shard_map/all_to_all | solution.py:69
  (71 shorter events, 24.3 us)
Async XLA Ops:
  7.2 276.2 %copy-start = (bf16[256,2048]{1,0:T(8,128)(2,1)S(1)}, bf16[256,2048]{1,0:T(8,128)(2,1)}, u32[]{:S(2)}) copy-start(bf16[256,2048]{1,0:T(8,128)(2,1)} %param.16) | copy-start | bytes 3145732
  7.2 4.8 %copy-start.13 = (s32[1,2]{1,0:T(1,128)S(1)}, s32[1,2]{1,0:T(1,128)}, u32[]{:S(2)}) copy-start(s32[1,2]{1,0:T(1,128)} %param.13) | copy-start | bytes 28
  7.2 11.0 %copy-start.10 = (bf16[1,2048]{1,0:T(2,128)(2,1)S(1)}, bf16[1,2048]{1,0:T(2,128)(2,1)}, u32[]{:S(2)}) copy-start(bf16[1,2048]{1,0:T(2,128)(2,1)} %param.15) | copy-start | bytes 12292
  7.2 40.6 %all-gather.6.cloned.1.call-start = ((), (), s32[]{:S(2)}) async-start(), calls=%async_computation.4 | async-start | bytes 5242880 | tf_op jit(solution)/shard_map/all_gather | solution.py:44
  10.5 164.4 %all-gather.10.cloned.1.call-start = ((), (), s32[]{:S(2)}) async-start(), calls=%async_computation.8 | async-start | bytes 9437184 | tf_op jit(solution)/shard_map/all_gather | solution.py:35
  11.2 197.9 %all-gather.8.cloned.1.call-start = ((), (), s32[]{:S(2)}) async-start(), calls=%async_computation.6 | async-start | bytes 5242880 | tf_op jit(solution)/shard_map/all_gather | solution.py:44
  12.0 271.4 %reduce-scatter.3.cloned.1.call-start = ((), (), s32[]{:S(2)}) async-start(), calls=%async_computation.5 | async-start | bytes 10485760 | tf_op jit(solution)/shard_map/reduce_scatter | solution.py:51
  189.5 168.2 %reduce-scatter.5.cloned.1.call-start = ((), (), s32[]{:S(2)}) async-start(), calls=%async_computation.7 | async-start | bytes 10485760 | tf_op jit(solution)/shard_map/reduce_scatter | solution.py:51
  209.2 3.4 copy-start.6
  226.2 0.8 copy-start.9
  226.2 1.7 copy-start.4
  226.2 2.3 copy-start.11
  228.6 1.6 copy-start.5
  230.2 53.1 %copy-start.2 = (bf16[1,1,16,16,2048]{4,3,2,1,0:T(8,128)(2,1)S(1)}, bf16[1,1,16,16,2048]{4,3,2,1,0:T(8,128)(2,1)}, u32[]{:S(2)}) copy-start(bf16[1,1,16,16,2048]{4,3,2,1,0:T(8,128)(2,1)} %get-tuple-element.8) | copy-start | bytes 3145732
  239.9 117.8 %copy-start.1 = (bf16[1,1,16,16,2048]{4,3,2,1,0:T(8,128)(2,1)S(1)}, bf16[1,1,16,16,2048]{4,3,2,1,0:T(8,128)(2,1)}, u32[]{:S(2)}) copy-start(bf16[1,1,16,16,2048]{4,3,2,1,0:T(8,128)(2,1)} %get-tuple-element.9) | copy-start | bytes 3145732
  357.7 3.1 copy-start.3
  361.2 8.8 %copy-start.8 = (bf16[256,2048]{1,0:T(8,128)(2,1)}, bf16[256,2048]{1,0:T(8,128)(2,1)S(1)}, u32[]{:S(2)}) copy-start(bf16[256,2048]{1,0:T(8,128)(2,1)S(1)} %get-tuple-element.15) | copy-start | bytes 3145732
  361.3 33.1 %copy-start.7 = (bf16[256,2048]{1,0:T(8,128)(2,1)}, bf16[256,2048]{1,0:T(8,128)(2,1)S(1)}, u32[]{:S(2)}) copy-start(bf16[256,2048]{1,0:T(8,128)(2,1)S(1)} %get-tuple-element.14) | copy-start | bytes 3145732
  388.8 33.0 %all-to-all-start.1 = ((bf16[8,2,32768]{2,1,0:T(2,128)(2,1)}), bf16[8,2,32768]{2,1,0:T(2,128)(2,1)S(1)}, u32[]{:S(2)}, u32[]{:S(2)}) async-start(bf16[8,2,32768]{2,1,0:T(2,128)(2,1)} %reshape.107), calls=%async_computation.3 | async-start | bytes 2097152 | tf_op jit(solution)/shard_map/all_to_all | solution.py:69
  410.6 17.2 %copy-start.12 = (bf16[1024]{0:T(1024)(128)(2,1)S(1)}, bf16[1024]{0:T(1024)(128)(2,1)}, u32[]{:S(2)}) copy-start(bf16[1024]{0:T(1024)(128)(2,1)} %param.19) | copy-start | bytes 6148
  421.8 31.4 %all-to-all-start = ((bf16[8,2,32768]{2,1,0:T(2,128)(2,1)}), bf16[8,2,32768]{2,1,0:T(2,128)(2,1)S(1)}, u32[]{:S(2)}, u32[]{:S(2)}) async-start(bf16[8,2,32768]{2,1,0:T(2,128)(2,1)} %reshape.109), calls=%async_computation.1 | async-start | bytes 2097152 | tf_op jit(solution)/shard_map/all_to_all | solution.py:69
Sparse Core Ops, SparseCore 0:
  10.6 37.1 all-gather.5
  49.9 124.9 all-gather.9
  176.5 32.6 all-gather.7
  211.6 71.7 reduce-scatter.2
  286.0 71.6 reduce-scatter.4
where the time goes:
time: 482 us; the launch traced here: 481 us
  waiting for transfers between devices  288 us (60%)
  local copies, waits for them, and re-layouts  97.5 us (20%)
  matrix products  52.9 us (11%)
  between operations  13.9 us (3%)
  starting transfers between devices  11.9 us (2%)
  other arithmetic  10.2 us (2%)
  blocking collectives  5.95 us (1%)
    all_gather x1, waiting for transfers between devices, local(): own_whole = lax.all_gather(weight_shard, 'env', axis=0, tiled=True)  124 us
    reduce_scatter x2, waiting for transfers between devices, local(): lax.psum_scatter(products, 'league', scatter_dimension=0, tiled=True)  114 us
    unnamed x39, local copies, waits for them, and re-layouts  57.8 us
    all_gather x2, waiting for transfers between devices, local(): all_rows = lax.all_gather(opp_raw, 'league', axis=0, tiled=True)  49.1 us
    dot_general x2, matrix products, local(): jnp.dot(all_normed, own_whole, preferred_element_type=jnp.float32)  28.1 us
    all_to_all x2, local copies, waits for them, and re-layouts, local(): lax.all_to_all(time_block, 'env', split_axis=1, concat_axis=2, tiled=True)  18.2 us
    reshape x2, local copies, waits for them, and re-layouts, local(): joint_row.reshape(env_count, step_count, model_width).transpose(1, 2, 0)  17.6 us
    all_to_all x2, starting transfers between devices, local(): lax.all_to_all(time_block, 'env', split_axis=1, concat_axis=2, tiled=True)  11.5 us
  transfers between devices with their start and end apart: 7, of which 5 were waited for; matrix products, arithmetic and copies ran while one was open for 21% of the time, Pallas kernels for 0%

commit v1 on v0

--- a/solution.py
+++ b/solution.py
@@ -32,7 +32,21 @@
     my_group = lax.axis_index("league")
     own_inputs = obs_own[0].reshape(round_count * row_count, model_width).astype(jnp.float32)
     own_normed = rms_norm(own_inputs, own_gain).astype(jnp.bfloat16)
-    own_whole = lax.all_gather(weight_shard, "env", axis=0, tiled=True)
+    ways, here, step = (lax.axis_size("env"), lax.axis_index("env"), weight_shard.shape[0])
+    dims = [n * ways if d == 0 else n for d, n in enumerate(weight_shard.shape)]
+    full = lax.dynamic_update_slice_in_dim(
+        jnp.zeros(dims, weight_shard.dtype), weight_shard, here * step, axis=0
+    )
+    going_up = going_down = weight_shard
+    for far in range(1, ways // 2 + 1):
+        going_up = lax.ppermute(going_up, "env", [(d, (d + 1) % ways) for d in range(ways)])
+        full = lax.dynamic_update_slice_in_dim(full, going_up, (here - far) % ways * step, axis=0)
+        if 2 * far < ways:
+            going_down = lax.ppermute(going_down, "env", [(d, (d - 1) % ways) for d in range(ways)])
+            full = lax.dynamic_update_slice_in_dim(
+                full, going_down, (here + far) % ways * step, axis=0
+            )
+    own_whole = full
     own_state = own_inputs + jnp.dot(own_normed, own_whole, preferred_element_type=jnp.float32)
     every_pick = lax.all_gather(opponent_picks, "league", axis=0, tiled=True)
     action_range = jnp.arange(action_table.shape[0], dtype=jnp.int32)

time: 482 us -> 467 us (0.969)
  waiting for transfers between devices: 288 us -> 236 us
  starting transfers between devices: 11.9 us -> 31.8 us
  local copies, waits for them, and re-layouts: 97.5 us -> 115 us
  other arithmetic: 10.2 us -> 16 us
  matrix products: 52.9 us -> 47.6 us
    ppermute x0 -> x7, waiting for transfers between devices: none -> 125 us  [the longest x4 125 us: local(): lax.ppermute(going_up, 'env', [(d, (d + 1) % ways) for d in range(ways)])]
    all_gather x1 -> x0, waiting for transfers between devices: 124 us -> none  [local(): own_whole = lax.all_gather(weight_shard, 'env', axis=0, tiled=True)]
    all_gather x2, waiting for transfers between devices: 49.1 us -> 0.02 us  [local(): all_rows = lax.all_gather(opp_raw, 'league', axis=0, tiled=True)]
    ppermute x0 -> x7, starting transfers between devices: none -> 20 us  [the longest x4 10.6 us: local(): lax.ppermute(going_up, 'env', [(d, (d + 1) % ways) for d in range(ways)])]
    dynamic_update_slice x0 -> x8, local copies, waits for them, and re-layouts: none -> 13.5 us  [the longest x4 8.06 us: local(): lax.dynamic_update_slice_in_dim(full, going_up, (here - far) % ways * ste...]
    reduce_sum x3 -> x4, other arithmetic: 6.75 us -> 12.5 us  [rms_norm(): scale = lax.rsqrt(jnp.mean(inputs * inputs, axis=-1, keepdims=True) + 1e-05)]
    unnamed x39 -> x41, local copies, waits for them, and re-layouts: 57.8 us -> 57.3 us
  transfers between devices with their start and end apart: 7 -> 13, of which waited for: 5 -> 7; matrix products, arithmetic and copies ran while one was open for 21% -> 25% of each run, Pallas kernels for 0% -> 0%
where the time goes in v1:
time: 467 us; the launch traced here: 466 us
  waiting for transfers between devices  236 us (51%)
  local copies, waits for them, and re-layouts  115 us (25%)
  matrix products  47.6 us (10%)
  starting transfers between devices  31.8 us (7%)
  other arithmetic  16 us (3%)
  between operations  14 us (3%)
  blocking collectives  5.03 us (1%)
    ppermute x4, waiting for transfers between devices, local(): lax.ppermute(going_up, 'env', [(d, (d + 1) % ways) for d in range(ways)])  125 us
    reduce_scatter x2, waiting for transfers between devices, local(): lax.psum_scatter(products, 'league', scatter_dimension=0, tiled=True)  111 us
    unnamed x41, local copies, waits for them, and re-layouts  57.3 us
    dot_general x2, matrix products, local(): jnp.dot(all_normed, own_whole, preferred_element_type=jnp.float32)  26.7 us
    all_to_all x2, local copies, waits for them, and re-layouts, local(): lax.all_to_all(time_block, 'env', split_axis=1, concat_axis=2, tiled=True)  18.2 us
    reshape x2, local copies, waits for them, and re-layouts, local(): joint_row.reshape(env_count, step_count, model_width).transpose(1, 2, 0)  17.6 us
    reduce_sum x4, other arithmetic, rms_norm(): scale = lax.rsqrt(jnp.mean(inputs * inputs, axis=-1, keepdims=True) + 1e-05)  12.5 us
    all_to_all x2, starting transfers between devices, local(): lax.all_to_all(time_block, 'env', split_axis=1, concat_axis=2, tiled=True)  11.5 us
  transfers between devices with their start and end apart: 13, of which 7 were waited for; matrix products, arithmetic and copies ran while one was open for 25% of the time, Pallas kernels for 0%

profile of v1, /device:TPU:0, one launch (start us, length us, event | category | flops | bytes accessed | tf_op | source)
XLA Modules:
  0.0 465.5 jit_solution(1026206039521137974)
XLA Ops:
  16.9 41.7 %collective-permute-done = bf16[256,2048]{1,0:T(8,128)(2,1)} collective-permute-done((bf16[256,2048]{1,0:T(8,128)(2,1)S(1)}, bf16[256,2048]{1,0:T(8,128)(2,1)}, u32[]{:S(2)}, u32[]{:S(2)}) %collective-permute-start) | collective-permute-done | bytes 1048608 | tf_op jit(solution)/shard_map/ppermute | solution.py:42
  64.2 5.0 %all-gather = s32[4,1,2]{2,1,0:T(1,128)S(1)} all-gather(s32[1,1,2]{2,1,0:T(1,128)S(1)} %bitcast.94), channel_id=1, replica_groups=mesh['league'=4,'env'=8] {'league'}, dimensions={0}, use_global_device_ids=true | all-gather | bytes 40 | tf_op jit(solution)/shard_map/all_gather | solution.py:51
  69.3 36.2 %collective-permute-done.2 = bf16[256,2048]{1,0:T(8,128)(2,1)} collective-permute-done((bf16[256,2048]{1,0:T(8,128)(2,1)}, bf16[256,2048]{1,0:T(8,128)(2,1)}, u32[]{:S(2)}, u32[]{:S(2)}) %collective-permute-start.2) | collective-permute-done | bytes 1048608 | tf_op jit(solution)/shard_map/ppermute | solution.py:42
  108.1 4.3 broadcast_in_dim.6
  119.1 32.6 %collective-permute-done.4 = bf16[256,2048]{1,0:T(8,128)(2,1)} collective-permute-done((bf16[256,2048]{1,0:T(8,128)(2,1)}, bf16[256,2048]{1,0:T(8,128)(2,1)}, u32[]{:S(2)}, u32[]{:S(2)}) %collective-permute-start.4) | collective-permute-done | bytes 1048608 | tf_op jit(solution)/shard_map/ppermute | solution.py:42
  163.3 14.3 %collective-permute-done.6 = bf16[256,2048]{1,0:T(8,128)(2,1)S(1)} collective-permute-done((bf16[256,2048]{1,0:T(8,128)(2,1)}, bf16[256,2048]{1,0:T(8,128)(2,1)S(1)}, u32[]{:S(2)}, u32[]{:S(2)}) %collective-permute-start.6) | collective-permute-done | bytes 1048608 | tf_op jit(solution)/shard_map/ppermute | solution.py:42
  182.1 13.3 %convolution_multiply_fusion = f32[1024,2048]{1,0:T(8,128)} fusion(bf16[2048,2048]{1,0:T(8,128)(2,1)} %constant_dynamic-update-slice_fusion, bf16[1024,2048]{1,0:T(8,128)(2,1)S(1)} %copy-done.7, f32[1024]{0:T(1024)S(1)} %bitcast.90, f32[1024]{0:T(1024)S(1)} %add_rsqrt_fusion.1, f32[2048]{0:T(1024)S(1)} %bitcast.86), kind=kOutput, calls=%fused_computation.10 | convolution fusion | flops 8600420352 | bytes 20987904 | tf_op jit(solution)/shard_map/dot_general | solution.py:60
  199.1 13.4 %convolution_multiply_fusion.1 = f32[1024,2048]{1,0:T(8,128)} fusion(bf16[2048,2048]{1,0:T(8,128)(2,1)} %constant_dynamic-update-slice_fusion, bf16[1024,2048]{1,0:T(8,128)(2,1)S(1)} %copy-done.6, f32[1024]{0:T(1024)S(1)} %bitcast.91, f32[2048]{0:T(1024)S(1)} %bitcast.87, f32[1024]{0:T(1024)S(1)} %add_rsqrt_fusion.2), kind=kOutput, calls=%fused_computation.11 | convolution fusion | flops 8600420352 | bytes 20987904 | tf_op jit(solution)/shard_map/dot_general | solution.py:60
  219.5 9.7 %bitcast_add_fusion = f32[512,2048]{1,0:T(8,128)} fusion(bf16[1,2,16,16,2048]{4,3,2,1,0:T(8,128)(2,1)S(1)} %copy-done.5, bf16[512,2048]{1,0:T(8,128)(2,1)S(1)} %fusion.10, bf16[2048,2048]{1,0:T(8,128)(2,1)} %constant_dynamic-update-slice_fusion), kind=kOutput, calls=%fused_computation.12 | convolution fusion | flops 4297064448 | bytes 16777216 | tf_op jit(solution)/shard_map/dot_general | solution.py:50
  229.2 36.6 %reduce-scatter.5.cloned.1.call-done = f32[256,2048]{1,0:T(8,128)} async-done(((f32[1024,2048]{1,0:T(8,128)}), f32[256,2048]{1,0:T(8,128)}) %reduce-scatter.5.cloned.1.call-update) | async-done | bytes 2097168 | tf_op jit(solution)/shard_map/reduce_scatter | solution.py:65
  265.7 74.4 %reduce-scatter.3.cloned.1.call-done = f32[256,2048]{1,0:T(8,128)} async-done(((f32[1024,2048]{1,0:T(8,128)}), f32[256,2048]{1,0:T(8,128)}) %reduce-scatter.3.cloned.1.call-update) | async-done | bytes 2097168 | tf_op jit(solution)/shard_map/reduce_scatter | solution.py:65
  340.1 5.6 %multiply_reduce_fusion.1 = (f32[256]{0:T(256)S(1)}, f32[256,2048]{1,0:T(8,128)S(1)}, f32[256]{0:T(256)S(1)}, f32[256,2048]{1,0:T(8,128)S(1)}) fusion(f32[256,2048]{1,0:T(8,128)} %fusion.28, f32[256,2048]{1,0:T(8,128)} %reduce-scatter.3.cloned.1.call-done, bf16[1,1,16,16,2048]{4,3,2,1,0:T(8,128)(2,1)S(1)} %copy-done.2, f32[512,2048]{1,0:T(8,128)} %bitcast_add_fusion, ...), kind=kLoop, calls=%fused_computation.30 | loop fusion | flops 6290944 | bytes 18876416 | tf_op jit(solution)/shard_map/reduce_sum | solution.py:8
  346.1 8.8 %copy.24 = bf16[16,16,2048]{0,1,2:T(8,128)(2,1)} copy(bf16[16,16,2048]{2,1,0:T(8,128)(2,1)S(1)} %bitcast.81) | data formatting | bytes 2097152 | tf_op jit(solution)/shard_map/reshape | solution.py:82
  354.9 7.5 %bitcast_bitcast_fusion.1 = bf16[2048,16,16]{2,1,0:T(8,128)(2,1)} fusion(bf16[16,16,2048]{0,1,2:T(8,128)(2,1)} %copy.24), kind=kLoop, calls=%fused_computation.76 | loop fusion | bytes 2097152
  362.4 11.2 %reshape.108 = bf16[8,2,32768]{2,1,0:T(2,128)(2,1)} reshape(bf16[2048,16,16]{2,1,0:T(8,128)(2,1)} %bitcast_bitcast_fusion.1) | data formatting | bytes 2097152
  373.7 5.5 %all-to-all-start = ((bf16[8,2,32768]{2,1,0:T(2,128)(2,1)}), bf16[8,2,32768]{2,1,0:T(2,128)(2,1)S(1)}, u32[]{:S(2)}, u32[]{:S(2)}) async-start(bf16[8,2,32768]{2,1,0:T(2,128)(2,1)} %reshape.108), calls=%async_computation.1 | async-start | bytes 2097152 | tf_op jit(solution)/shard_map/all_to_all | solution.py:83
  379.2 8.8 %copy.27 = bf16[16,16,2048]{0,1,2:T(8,128)(2,1)} copy(bf16[16,16,2048]{2,1,0:T(8,128)(2,1)S(1)} %bitcast.80) | data formatting | bytes 2097152 | tf_op jit(solution)/shard_map/reshape | solution.py:82
  388.0 7.5 %bitcast_bitcast_fusion = bf16[2048,16,16]{2,1,0:T(8,128)(2,1)} fusion(bf16[16,16,2048]{0,1,2:T(8,128)(2,1)} %copy.27), kind=kLoop, calls=%fused_computation.75 | loop fusion | bytes 2097152
  395.5 11.3 %reshape.106 = bf16[8,2,32768]{2,1,0:T(2,128)(2,1)} reshape(bf16[2048,16,16]{2,1,0:T(8,128)(2,1)} %bitcast_bitcast_fusion) | data formatting | bytes 2097152
  406.7 6.0 %all-to-all-start.1 = ((bf16[8,2,32768]{2,1,0:T(2,128)(2,1)}), bf16[8,2,32768]{2,1,0:T(2,128)(2,1)S(1)}, u32[]{:S(2)}, u32[]{:S(2)}) async-start(bf16[8,2,32768]{2,1,0:T(2,128)(2,1)} %reshape.106), calls=%async_computation.3 | async-start | bytes 2097152 | tf_op jit(solution)/shard_map/all_to_all | solution.py:83
  421.2 7.5 %reshape.109 = bf16[2048,16,16]{2,1,0:T(8,128)(2,1)} reshape(bf16[8,2,32768]{2,1,0:T(2,128)(2,1)S(1)} %all-to-all-done) | data formatting | bytes 2097152
  428.7 9.1 %copy.26 = bf16[16,256,8,16]{1,3,2,0:T(8,128)(2,1)} copy(bf16[16,256,8,16]{3,0,1,2:T(8,128)(2,1)} %bitcast.76) | data formatting | bytes 2097152 | tf_op jit(solution)/shard_map/all_to_all | solution.py:83
  438.1 7.5 %reshape.107 = bf16[2048,16,16]{2,1,0:T(8,128)(2,1)} reshape(bf16[8,2,32768]{2,1,0:T(2,128)(2,1)S(1)} %all-to-all-done.1) | data formatting | bytes 2097152
  445.7 9.1 %copy.29 = bf16[16,256,8,16]{1,3,2,0:T(8,128)(2,1)} copy(bf16[16,256,8,16]{3,0,1,2:T(8,128)(2,1)} %bitcast.77) | data formatting | bytes 2097152 | tf_op jit(solution)/shard_map/all_to_all | solution.py:83
  (94 shorter events, 64.6 us)
Async XLA Ops:
  7.2 207.9 %copy-start = (bf16[256,2048]{1,0:T(8,128)(2,1)S(1)}, bf16[256,2048]{1,0:T(8,128)(2,1)}, u32[]{:S(2)}) copy-start(bf16[256,2048]{1,0:T(8,128)(2,1)} %param.16) | copy-start | bytes 3145732
  7.2 3.5 copy-start.9
  7.2 57.0 %copy-start.14 = (s32[1,2]{1,0:T(1,128)S(1)}, s32[1,2]{1,0:T(1,128)}, u32[]{:S(2)}) copy-start(s32[1,2]{1,0:T(1,128)} %param.13) | copy-start | bytes 28
  7.2 100.9 %copy-start.11 = (bf16[1,2048]{1,0:T(2,128)(2,1)S(1)}, bf16[1,2048]{1,0:T(2,128)(2,1)}, u32[]{:S(2)}) copy-start(bf16[1,2048]{1,0:T(2,128)(2,1)} %param.15) | copy-start | bytes 12292
  7.2 171.4 %all-gather.6.cloned.1.call-start = ((), (), s32[]{:S(2)}) async-start(), calls=%async_computation.6 | async-start | bytes 5242880 | tf_op jit(solution)/shard_map/all_gather | solution.py:58
  10.6 185.1 %all-gather.4.cloned.1.call-start = ((), (), s32[]{:S(2)}) async-start(), calls=%async_computation.4 | async-start | bytes 5242880 | tf_op jit(solution)/shard_map/all_gather | solution.py:58
  10.7 47.9 %collective-permute-start = (bf16[256,2048]{1,0:T(8,128)(2,1)S(1)}, bf16[256,2048]{1,0:T(8,128)(2,1)}, u32[]{:S(2)}, u32[]{:S(2)}) collective-permute-start(bf16[256,2048]{1,0:T(8,128)(2,1)S(1)} %bitcast.84), channel_id=1, source_target_pairs={{0,1},{1,2},{2,3},{3,4},{4,5},{5,6},{6,7},{7,0},{8,9},{9,10},{10,1... | collective-permute-start | bytes 3145736 | tf_op jit(solution)/shard_map/ppermute | solution.py:42
  13.7 47.5 %collective-permute-start.1 = (bf16[256,2048]{1,0:T(8,128)(2,1)S(1)}, bf16[256,2048]{1,0:T(8,128)(2,1)S(1)}, u32[]{:S(2)}, u32[]{:S(2)}) collective-permute-start(bf16[256,2048]{1,0:T(8,128)(2,1)S(1)} %bitcast.85), channel_id=1, source_target_pairs={{0,7},{1,0},{2,1},{3,2},{4,3},{5,4},{6,5},{7,6},{8,15},{9,8},{10,9... | collective-permute-start | bytes 3145736 | tf_op jit(solution)/shard_map/ppermute | solution.py:45
  16.8 248.9 %reduce-scatter.5.cloned.1.call-start = ((), (), s32[]{:S(2)}) async-start(), calls=%async_computation.7 | async-start | bytes 10485760 | tf_op jit(solution)/shard_map/reduce_scatter | solution.py:65
  58.6 46.9 %collective-permute-start.2 = (bf16[256,2048]{1,0:T(8,128)(2,1)}, bf16[256,2048]{1,0:T(8,128)(2,1)}, u32[]{:S(2)}, u32[]{:S(2)}) collective-permute-start(bf16[256,2048]{1,0:T(8,128)(2,1)} %collective-permute-done), channel_id=1, source_target_pairs={{0,1},{1,2},{2,3},{3,4},{4,5},{5,6},{6,7},{7,0},{8,9},{9,10},{10,1... | collective-permute-start | bytes 3145736 | tf_op jit(solution)/shard_map/ppermute | solution.py:42
  61.2 52.3 %collective-permute-start.3 = (bf16[256,2048]{1,0:T(8,128)(2,1)S(1)}, bf16[256,2048]{1,0:T(8,128)(2,1)}, u32[]{:S(2)}, u32[]{:S(2)}) collective-permute-start(bf16[256,2048]{1,0:T(8,128)(2,1)S(1)} %collective-permute-done.1), channel_id=1, source_target_pairs={{0,7},{1,0},{2,1},{3,2},{4,3},{5,4},{6,5},{7,6},{8,15},{9,8},{10,9... | collective-permute-start | bytes 3145736 | tf_op jit(solution)/shard_map/ppermute | solution.py:45
  105.5 46.3 %collective-permute-start.4 = (bf16[256,2048]{1,0:T(8,128)(2,1)}, bf16[256,2048]{1,0:T(8,128)(2,1)}, u32[]{:S(2)}, u32[]{:S(2)}) collective-permute-start(bf16[256,2048]{1,0:T(8,128)(2,1)} %collective-permute-done.2), channel_id=1, source_target_pairs={{0,1},{1,2},{2,3},{3,4},{4,5},{5,6},{6,7},{7,0},{8,9},{9,10},{10,1... | collective-permute-start | bytes 3145736 | tf_op jit(solution)/shard_map/ppermute | solution.py:42
  113.5 48.7 %collective-permute-start.5 = (bf16[256,2048]{1,0:T(8,128)(2,1)}, bf16[256,2048]{1,0:T(8,128)(2,1)S(1)}, u32[]{:S(2)}, u32[]{:S(2)}) collective-permute-start(bf16[256,2048]{1,0:T(8,128)(2,1)} %collective-permute-done.3), channel_id=1, source_target_pairs={{0,7},{1,0},{2,1},{3,2},{4,3},{5,4},{6,5},{7,6},{8,15},{9,8},{10,9... | collective-permute-start | bytes 3145736 | tf_op jit(solution)/shard_map/ppermute | solution.py:45
  151.8 25.8 %collective-permute-start.6 = (bf16[256,2048]{1,0:T(8,128)(2,1)}, bf16[256,2048]{1,0:T(8,128)(2,1)S(1)}, u32[]{:S(2)}, u32[]{:S(2)}) collective-permute-start(bf16[256,2048]{1,0:T(8,128)(2,1)} %collective-permute-done.4), channel_id=1, source_target_pairs={{0,1},{1,2},{2,3},{3,4},{4,5},{5,6},{6,7},{7,0},{8,9},{9,10},{10,1... | collective-permute-start | bytes 3145736 | tf_op jit(solution)/shard_map/ppermute | solution.py:42
  178.6 3.4 copy-start.7
  195.4 144.7 %reduce-scatter.3.cloned.1.call-start = ((), (), s32[]{:S(2)}) async-start(), calls=%async_computation.5 | async-start | bytes 10485760 | tf_op jit(solution)/shard_map/reduce_scatter | solution.py:65
  195.7 3.5 copy-start.6
  219.5 120.6 %copy-start.2 = (bf16[1,1,16,16,2048]{4,3,2,1,0:T(8,128)(2,1)S(1)}, bf16[1,1,16,16,2048]{4,3,2,1,0:T(8,128)(2,1)}, u32[]{:S(2)}) copy-start(bf16[1,1,16,16,2048]{4,3,2,1,0:T(8,128)(2,1)} %get-tuple-element.14) | copy-start | bytes 3145732
  219.5 120.6 %copy-start.3 = (bf16[1,1,16,16,2048]{4,3,2,1,0:T(8,128)(2,1)S(1)}, bf16[1,1,16,16,2048]{4,3,2,1,0:T(8,128)(2,1)}, u32[]{:S(2)}) copy-start(bf16[1,1,16,16,2048]{4,3,2,1,0:T(8,128)(2,1)} %get-tuple-element.15) | copy-start | bytes 3145732
  346.1 8.8 %copy-start.8 = (bf16[256,2048]{1,0:T(8,128)(2,1)}, bf16[256,2048]{1,0:T(8,128)(2,1)S(1)}, u32[]{:S(2)}) copy-start(bf16[256,2048]{1,0:T(8,128)(2,1)S(1)} %get-tuple-element.20) | copy-start | bytes 3145732
  373.7 33.1 %all-to-all-start = ((bf16[8,2,32768]{2,1,0:T(2,128)(2,1)}), bf16[8,2,32768]{2,1,0:T(2,128)(2,1)S(1)}, u32[]{:S(2)}, u32[]{:S(2)}) async-start(bf16[8,2,32768]{2,1,0:T(2,128)(2,1)} %reshape.108), calls=%async_computation.1 | async-start | bytes 2097152 | tf_op jit(solution)/shard_map/all_to_all | solution.py:83
  395.5 17.3 %copy-start.13 = (bf16[1024]{0:T(1024)(128)(2,1)S(1)}, bf16[1024]{0:T(1024)(128)(2,1)}, u32[]{:S(2)}) copy-start(bf16[1024]{0:T(1024)(128)(2,1)} %param.19) | copy-start | bytes 6148
  406.7 31.4 %all-to-all-start.1 = ((bf16[8,2,32768]{2,1,0:T(2,128)(2,1)}), bf16[8,2,32768]{2,1,0:T(2,128)(2,1)S(1)}, u32[]{:S(2)}, u32[]{:S(2)}) async-start(bf16[8,2,32768]{2,1,0:T(2,128)(2,1)} %reshape.106), calls=%async_computation.3 | async-start | bytes 2097152 | tf_op jit(solution)/shard_map/all_to_all | solution.py:83
  454.8 4.2 copy-start.1
  (4 other events, 8.9 us)
Sparse Core Ops, SparseCore 0:
  10.7 37.1 all-gather.5
  49.5 34.4 all-gather.3
  195.5 70.1 reduce-scatter.4
  268.3 71.7 reduce-scatter.2
